TPU v7x, 512 devices: a whole 4x8x8 slice. The times are simulated.
512 devices in a mesh: snap: 32 (over x_hi, y, core), var: 16 (over z, x_lo).
Axes of the slice: x: 4 (x_hi: 2, x_lo: 2; x = x_hi * 2 + x_lo), y: 8, z: 8, core: 2. Of those that a mesh axis runs over, the one named last changes fastest.
Arguments:
- tensor: float32 [512, 1280, 1024], P('var', 'snap'), may hold values from 0.05 to 5
- cell_factor: float32 [1024, 256], P('snap'), may hold values from 0.1 to 1
- var_factor: float32 [512, 256], P('var'), may hold values from 0.1 to 1
- snap_factor: float32 [1280, 256], P('snap'), may hold values from 0.002 to 0.02
Outputs:
- grad_cells: float32 [1024, 256], P('snap')
- grad_vars: float32 [512, 256], P('var')
- grad_snaps: float32 [1280, 256], P('snap')
All inputs are finite; a program needn't handle non-finite values.
Results may differ from a plain program's by a relative error of at most 0.0003.
Values sent between devices are 32-bit elements; how exact they have to be, the bound alone decides.
No kernel may reach another device: no remote copies, remote signals or barrier semaphores. Data moves between devices by JAX's collectives and lax.ppermute only.
A program may use at most 64 MiB of HBM per device.

v0:
```python
import jax
import jax.numpy as jnp
from jax import lax
from jax.sharding import PartitionSpec as P

high = lax.Precision.HIGHEST


def local(tensor, cell_factor, var_factor, snap_factor):
    var_rows, snap_rows, cells = tensor.shape
    rank = cell_factor.shape[1]
    khatri = (var_factor[:, None, :] * snap_factor[None, :, :]).reshape(var_rows * snap_rows, rank)
    flat = tensor.reshape(var_rows * snap_rows, cells)
    all_cells = lax.all_gather(cell_factor, "snap", axis=0, tiled=True)
    model = jnp.dot(khatri, all_cells.T, precision=high, preferred_element_type=jnp.float32)
    deriv = (model - flat) * lax.rsqrt(model)
    partial_cells = jnp.dot(deriv.T, khatri, precision=high, preferred_element_type=jnp.float32)
    folded = jnp.dot(deriv, all_cells, precision=high, preferred_element_type=jnp.float32).reshape(
        var_rows, snap_rows, rank
    )
    partial_vars = jnp.einsum("vsr,sr->vr", folded, snap_factor, precision=high)
    partial_snaps = jnp.einsum("vsr,vr->sr", folded, var_factor, precision=high)
    summed = lax.psum(partial_cells, "var")
    grad_cells = lax.psum_scatter(summed, "snap", scatter_dimension=0, tiled=True)
    grad_vars = lax.psum(partial_vars, "snap")
    grad_snaps = lax.psum(partial_snaps, "var")
    return (grad_cells, grad_vars, grad_snaps)


def solution(mesh):
    placed = (P("var", "snap", None), P("snap", None), P("var", None), P("snap", None))
    return jax.shard_map(
        local,
        mesh=mesh,
        in_specs=placed,
        out_specs=(P("snap", None), P("var", None), P("snap", None)),
        check_vma=False,
    )
```

profile of v0, /device:TPU:6, one launch (start us, length us, event | category | flops | bytes accessed | tf_op | source)
XLA Modules:
  0.0 389.5 jit_solution(5850247747479945227)
XLA Ops:
  7.2 0.0 all-gather.2.cloned.1.call-start
  7.2 0.7 all-gather.2.cloned.1.call-update
  7.9 0.0 reduce-scatter.2.cloned.1.call-start
  7.9 0.9 broadcast_multiply_fusion
  8.8 88.6 %all-gather.2.cloned.1.call-done = f32[1024,256]{1,0:T(8,128)} async-done(((f32[32,256]{1,0:T(8,128)}), f32[1024,256]{1,0:T(8,128)}) %all-gather.2.cloned.1.call-update) | async-done | bytes 1048592 | tf_op jit(solution)/shard_map/all_gather | solution.py:14
  97.4 6.9 %fusion = f32[1280,1024]{1,0:T(8,128)S(1)} fusion(f32[32,40,1024]{2,1,0:T(8,128)} %param.4, f32[1280,256]{1,0:T(8,128)S(1)} %bitcast.20, f32[1024,256]{1,0:T(8,128)} %all-gather.2.cloned.1.call-done), kind=kOutput, calls=%fused_computation.1 | convolution fusion | flops 4029153280 | bytes 12845056 | tf_op jit(solution)/shard_map/dot_general | solution.py:15
  104.4 2.3 copy-done
  106.7 9.6 %fusion.1 = f32[1024,256]{1,0:T(8,128)} fusion(f32[1280,1024]{1,0:T(8,128)S(1)} %fusion, f32[1280,256]{1,0:T(8,128)S(1)} %bitcast.21), kind=kOutput, calls=%fused_computation.5 | convolution fusion | flops 4026531840 | bytes 7602176 | tf_op jit(solution)/shard_map/dot_general | solution.py:17
  116.2 0.0 reduce-scatter.2.cloned.1.call-update
  116.3 0.0 copy-start.3
  116.3 0.2 all-reduce.3.cloned.1.call-start
  116.5 1.0 copy-done.1
  117.5 6.2 %fusion.2 = f32[1280,256]{1,0:T(8,128)S(1)} fusion(f32[1280,1024]{1,0:T(8,128)} %copy-done, f32[1024,256]{1,0:T(8,128)S(1)} %copy-done.1), kind=kOutput, calls=%fused_computation.6 | convolution fusion | flops 4026531840 | bytes 7602176 | tf_op jit(solution)/shard_map/dot_general | solution.py:18
  123.7 0.0 copy-start.2
  123.7 0.0 copy-done.3
  123.7 0.7 multiply_reduce_fusion
  124.4 113.6 %reduce-scatter.2.cloned.1.call-done = f32[32,256]{1,0:T(8,128)} async-done(((f32[1024,256]{1,0:T(8,128)}), f32[32,256]{1,0:T(8,128)}) %reduce-scatter.2.cloned.1.call-update) | async-done | bytes 32784 | tf_op jit(solution)/shard_map/reduce_scatter | solution.py:24
  238.0 0.0 all-reduce.3.cloned.1.call-update
  238.1 0.0 copy-done.2
  238.1 0.1 multiply_reduce_fusion.1
  238.2 129.1 %psum.22 = f32[32,256]{1,0:T(8,128)} all-reduce(f32[32,256]{1,0:T(8,128)S(1)} %bitcast.27), channel_id=1, replica_groups=mesh['snap'=32,'var'=16] {'snap'}, use_global_device_ids=true, to_apply=%region_2.0 | all-reduce | flops 8192 | bytes 65536 | tf_op jit(solution)/shard_map/psum | solution.py:25
  367.3 12.8 %all-reduce.3.cloned.1.call-done = (f32[32,256]{1,0:T(8,128)}, f32[40,256]{1,0:T(8,128)}) async-done(((f32[32,256]{1,0:T(8,128)}, f32[40,256]{1,0:T(8,128)}), (f32[32,256]{1,0:T(8,128)}, f32[40,256]{1,0:T(8,128)})) %all-reduce.3.cloned.1.call-update) | async-done | bytes 73744 | tf_op jit(solution)/shard_map/psum | solution.py:23
  380.2 1.4 copy.23
  381.5 1.4 copy.24
  (2 shorter events, 0.0 us)
Async XLA Ops:
  7.2 90.3 %all-gather.2.cloned.1.call-start = ((), (), s32[]{:S(2)}) async-start(), calls=%async_computation.1 | async-start | bytes 1081344 | tf_op jit(solution)/shard_map/all_gather | solution.py:14
  7.9 230.1 %reduce-scatter.2.cloned.1.call-start = ((), (), s32[]{:S(2)}) async-start(), calls=%async_computation.2 | async-start | bytes 1081344 | tf_op jit(solution)/shard_map/reduce_scatter | solution.py:24
  104.4 2.3 copy-start
  116.2 1.2 copy-start.1
  116.3 7.4 %copy-start.3 = (f32[32,256]{1,0:T(8,128)S(1)}, f32[32,256]{1,0:T(8,128)}, u32[]{:S(2)}) copy-start(f32[32,256]{1,0:T(8,128)} %param.6) | copy-start | bytes 98308
  116.3 263.9 %all-reduce.3.cloned.1.call-start = ((), (), s32[]{:S(2)}) async-start(), calls=%async_computation.3 | async-start | bytes 147456 | tf_op jit(solution)/shard_map/psum | solution.py:23
  123.7 114.4 %copy-start.2 = (f32[40,256]{1,0:T(8,128)S(1)}, f32[40,256]{1,0:T(8,128)}, u32[]{:S(2)}) copy-start(f32[40,256]{1,0:T(8,128)} %param.7) | copy-start | bytes 122884
Sparse Core Ops, SparseCore 0:
  11.3 86.0 all-gather.1
  116.4 121.6 reduce-scatter.1
  241.6 138.5 all-reduce.2
where the time goes:
time: 390 us; the launch traced here: 389 us
  waiting for transfers between devices  216 us (55%)
  blocking collectives  129 us (33%)
  matrix products  22.7 us (6%)
  between operations  13.8 us (4%)
  local copies, waits for them, and re-layouts  6.04 us (2%)
    psum x1, blocking collectives, local(): grad_vars = lax.psum(partial_vars, 'snap')  129 us
    reduce_scatter x1, waiting for transfers between devices, local(): lax.psum_scatter(summed, 'snap', scatter_dimension=0, tiled=True)  114 us
    all_gather x1, waiting for transfers between devices, local(): all_cells = lax.all_gather(cell_factor, 'snap', axis=0, tiled=True)  88.6 us
    psum x1, waiting for transfers between devices, local(): summed = lax.psum(partial_cells, 'var')  12.8 us
    dot_general x1, matrix products, local(): jnp.dot(deriv.T, khatri, precision=high, preferred_element_type=jnp.float32)  9.55 us
  transfers between devices with their start and end apart: 3, of which 3 were waited for; matrix products, arithmetic and copies ran while one was open for 2% of the time, Pallas kernels for 0%

commit v1 on v0

--- a/solution.py
+++ b/solution.py
@@ -4,6 +4,12 @@
 from jax.sharding import PartitionSpec as P
 
 high = lax.Precision.HIGHEST
+
+
+def add_all(x, axis):
+    pieces = lax.all_gather(x, axis, axis=0, tiled=False)
+    total = pieces.sum(axis=0)
+    return total
 
 
 def local(tensor, cell_factor, var_factor, snap_factor):
@@ -22,7 +28,7 @@
     partial_snaps = jnp.einsum("vsr,vr->sr", folded, var_factor, precision=high)
     summed = lax.psum(partial_cells, "var")
     grad_cells = lax.psum_scatter(summed, "snap", scatter_dimension=0, tiled=True)
-    grad_vars = lax.psum(partial_vars, "snap")
+    grad_vars = add_all(partial_vars, "snap")
     grad_snaps = lax.psum(partial_snaps, "var")
     return (grad_cells, grad_vars, grad_snaps)
 

time: 390 us -> 474 us (1.22)
  waiting for transfers between devices: 216 us -> 426 us
  blocking collectives: 129 us -> 0 us
    psum x1 -> x0, blocking collectives: 129 us -> none  [local(): grad_vars = lax.psum(partial_vars, 'snap')]
    psum x1, waiting for transfers between devices: 12.8 us -> 139 us  [local(): summed = lax.psum(partial_cells, 'var')]
    all_gather x0 -> x1, waiting for transfers between devices: none -> 85.1 us  [add_all(): pieces = lax.all_gather(x, axis, axis=0, tiled=False)]
  transfers between devices with their start and end apart: 3 -> 4, of which waited for: 3 -> 4; matrix products, arithmetic and copies ran while one was open for 2% -> 2% of each run, Pallas kernels for 0% -> 0%
where the time goes in v1:
time: 474 us; the launch traced here: 473 us
  waiting for transfers between devices  426 us (90%)
  matrix products  22.7 us (5%)
  between operations  13.8 us (3%)
  local copies, waits for them, and re-layouts  6.03 us (1%)
    psum x1, waiting for transfers between devices, local(): summed = lax.psum(partial_cells, 'var')  139 us
    reduce_scatter x1, waiting for transfers between devices, local(): lax.psum_scatter(summed, 'snap', scatter_dimension=0, tiled=True)  113 us
    all_gather x1, waiting for transfers between devices, local(): all_cells = lax.all_gather(cell_factor, 'snap', axis=0, tiled=True)  88.6 us
    all_gather x1, waiting for transfers between devices, add_all(): pieces = lax.all_gather(x, axis, axis=0, tiled=False)  85.1 us
    dot_general x1, matrix products, local(): jnp.dot(deriv.T, khatri, precision=high, preferred_element_type=jnp.float32)  9.55 us
  transfers between devices with their start and end apart: 4, of which 4 were waited for; matrix products, arithmetic and copies ran while one was open for 2% of the time, Pallas kernels for 0%

profile of v1, /device:TPU:6, one launch (start us, length us, event | category | flops | bytes accessed | tf_op | source)
XLA Modules:
  0.0 473.4 jit_solution(3849814898418604008)
XLA Ops:
  7.2 0.0 all-gather.4.cloned.1.call-start
  7.2 0.7 all-gather.4.cloned.1.call-update
  7.9 0.0 reduce-scatter.2.cloned.1.call-start
  7.9 0.9 broadcast_multiply_fusion
  8.8 88.6 %all-gather.4.cloned.1.call-done = f32[1024,256]{1,0:T(8,128)} async-done(((f32[32,256]{1,0:T(8,128)}), f32[1024,256]{1,0:T(8,128)}) %all-gather.4.cloned.1.call-update) | async-done | bytes 1048592 | tf_op jit(solution)/shard_map/all_gather | solution.py:20
  97.4 6.9 %fusion = f32[1280,1024]{1,0:T(8,128)S(1)} fusion(f32[32,40,1024]{2,1,0:T(8,128)} %param.4, f32[1280,256]{1,0:T(8,128)S(1)} %bitcast.21, f32[1024,256]{1,0:T(8,128)} %all-gather.4.cloned.1.call-done), kind=kOutput, calls=%fused_computation.1 | convolution fusion | flops 4029153280 | bytes 12845056 | tf_op jit(solution)/shard_map/dot_general | solution.py:21
  104.4 2.3 copy-done
  106.7 9.6 %fusion.1 = f32[1024,256]{1,0:T(8,128)} fusion(f32[1280,1024]{1,0:T(8,128)S(1)} %fusion, f32[1280,256]{1,0:T(8,128)S(1)} %bitcast.22), kind=kOutput, calls=%fused_computation.5 | convolution fusion | flops 4026531840 | bytes 7602176 | tf_op jit(solution)/shard_map/dot_general | solution.py:23
  116.2 0.0 reduce-scatter.2.cloned.1.call-update
  116.2 0.0 copy-start.2
  116.3 0.2 all-gather.6.cloned.1.call-start
  116.5 1.0 copy-done.1
  117.4 6.2 %fusion.2 = f32[1280,256]{1,0:T(8,128)S(1)} fusion(f32[1280,1024]{1,0:T(8,128)} %copy-done, f32[1024,256]{1,0:T(8,128)S(1)} %copy-done.1), kind=kOutput, calls=%fused_computation.6 | convolution fusion | flops 4026531840 | bytes 7602176 | tf_op jit(solution)/shard_map/dot_general | solution.py:24
  123.7 0.8 multiply_reduce_fusion.1
  124.4 0.0 all-gather.6.cloned.1.call-update
  124.4 0.0 all-reduce.3.cloned.1.call-start
  124.5 0.7 multiply_reduce_fusion
  125.3 112.8 %reduce-scatter.2.cloned.1.call-done = f32[32,256]{1,0:T(8,128)} async-done(((f32[1024,256]{1,0:T(8,128)}), f32[32,256]{1,0:T(8,128)}) %reduce-scatter.2.cloned.1.call-update) | async-done | bytes 32784 | tf_op jit(solution)/shard_map/reduce_scatter | solution.py:30
  238.0 0.0 all-reduce.3.cloned.1.call-update
  238.0 85.1 %all-gather.6.cloned.1.call-done = f32[1024,256]{1,0:T(8,128)} async-done(((f32[32,256]{1,0:T(8,128)}), f32[1024,256]{1,0:T(8,128)}) %all-gather.6.cloned.1.call-update) | async-done | bytes 1048592 | tf_op jit(solution)/shard_map/all_gather | solution.py:10
  323.2 1.9 reduce_sum.9
  325.1 139.0 %all-reduce.3.cloned.1.call-done = (f32[32,256]{1,0:T(8,128)}, f32[40,256]{1,0:T(8,128)}) async-done(((f32[32,256]{1,0:T(8,128)}, f32[40,256]{1,0:T(8,128)}), (f32[32,256]{1,0:T(8,128)}, f32[40,256]{1,0:T(8,128)})) %all-reduce.3.cloned.1.call-update) | async-done | bytes 73744 | tf_op jit(solution)/shard_map/psum | solution.py:29
  464.1 1.4 copy.23
  465.5 1.4 copy.24
  (5 shorter events, 0.0 us)
Async XLA Ops:
  7.2 90.3 %all-gather.4.cloned.1.call-start = ((), (), s32[]{:S(2)}) async-start(), calls=%async_computation.1 | async-start | bytes 1081344 | tf_op jit(solution)/shard_map/all_gather | solution.py:20
  7.9 230.1 %reduce-scatter.2.cloned.1.call-start = ((), (), s32[]{:S(2)}) async-start(), calls=%async_computation.3 | async-start | bytes 1081344 | tf_op jit(solution)/shard_map/reduce_scatter | solution.py:30
  104.4 2.3 copy-start
  116.2 1.2 copy-start.1
  116.2 7.4 %copy-start.2 = (f32[40,256]{1,0:T(8,128)S(1)}, f32[40,256]{1,0:T(8,128)}, u32[]{:S(2)}) copy-start(f32[40,256]{1,0:T(8,128)} %param.7) | copy-start | bytes 122884
  116.3 206.9 %all-gather.6.cloned.1.call-start = ((), (), s32[]{:S(2)}) async-start(), calls=%async_computation.2 | async-start | bytes 1081344 | tf_op jit(solution)/shard_map/all_gather | solution.py:10
  123.6 0.9 copy-start.3
  124.4 339.6 %all-reduce.3.cloned.1.call-start = ((), (), s32[]{:S(2)}) async-start(), calls=%async_computation.4 | async-start | bytes 147456 | tf_op jit(solution)/shard_map/psum | solution.py:29
Sparse Core Ops, SparseCore 0:
  11.3 86.0 all-gather.3
  116.4 121.6 reduce-scatter.1
  242.0 81.1 all-gather.5
  326.6 137.4 all-reduce.2

commit v2 on v0

--- a/solution.py
+++ b/solution.py
@@ -11,7 +11,15 @@
     rank = cell_factor.shape[1]
     khatri = (var_factor[:, None, :] * snap_factor[None, :, :]).reshape(var_rows * snap_rows, rank)
     flat = tensor.reshape(var_rows * snap_rows, cells)
-    all_cells = lax.all_gather(cell_factor, "snap", axis=0, tiled=True)
+    all_cells = jnp.concatenate(
+        jax.lax.all_to_all(
+            jnp.stack([cell_factor] * jax.lax.axis_size("snap"), axis=0),
+            split_axis=0,
+            concat_axis=0,
+            axis_name="snap",
+        ),
+        0,
+    )
     model = jnp.dot(khatri, all_cells.T, precision=high, preferred_element_type=jnp.float32)
     deriv = (model - flat) * lax.rsqrt(model)
     partial_cells = jnp.dot(deriv.T, khatri, precision=high, preferred_element_type=jnp.float32)

time: 390 us -> 342 us (0.88)
  waiting for transfers between devices: 216 us -> 157 us
  starting transfers between devices: 0.3 us -> 10.6 us
    all_gather x1 -> x0, waiting for transfers between devices: 88.6 us -> none  [local(): all_cells = lax.all_gather(cell_factor, 'snap', axis=0, tiled=True)]
    all_to_all x0 -> x1, waiting for transfers between devices: none -> 27.2 us  [local(): jax.lax.all_to_all(jnp.stack([cell_factor] * jax.lax.axis_size('snap'), a...]
    all_to_all x0 -> x1, starting transfers between devices: none -> 10.4 us  [local(): jax.lax.all_to_all(jnp.stack([cell_factor] * jax.lax.axis_size('snap'), a...]
where the time goes in v2:
time: 342 us; the launch traced here: 341 us
  waiting for transfers between devices  157 us (46%)
  blocking collectives  129 us (38%)
  matrix products  23 us (7%)
  between operations  14.1 us (4%)
  starting transfers between devices  10.6 us (3%)
  local copies, waits for them, and re-layouts  6.95 us (2%)
    psum x1, blocking collectives, local(): grad_vars = lax.psum(partial_vars, 'snap')  129 us
    reduce_scatter x1, waiting for transfers between devices, local(): lax.psum_scatter(summed, 'snap', scatter_dimension=0, tiled=True)  117 us
    all_to_all x1, waiting for transfers between devices, local(): jax.lax.all_to_all(jnp.stack([cell_factor] * jax.lax.axis_size('snap'), a...  27.2 us
    psum x1, waiting for transfers between devices, local(): summed = lax.psum(partial_cells, 'var')  12.9 us
    all_to_all x1, starting transfers between devices, local(): jax.lax.all_to_all(jnp.stack([cell_factor] * jax.lax.axis_size('snap'), a...  10.4 us
    dot_general x1, matrix products, local(): jnp.dot(deriv.T, khatri, precision=high, preferred_element_type=jnp.float32)  9.57 us
  transfers between devices with their start and end apart: 3, of which 3 were waited for; matrix products, arithmetic and copies ran while one was open for 2% of the time, Pallas kernels for 0%

profile of v2, /device:TPU:6, one launch (start us, length us, event | category | flops | bytes accessed | tf_op | source)
XLA Modules:
  0.0 341.2 jit_solution(556202444231684559)
XLA Ops:
  7.2 1.9 stack.2
  9.0 0.0 copy-start.1
  9.0 0.0 copy-start.2
  9.0 10.4 %all-to-all-start = ((f32[32,32,256]{2,1,0:T(8,128)}), f32[32,32,256]{2,1,0:T(8,128)S(1)}, u32[]{:S(2)}, u32[]{:S(2)}) async-start(f32[32,32,256]{2,1,0:T(8,128)} %stack.2), calls=%async_computation | async-start | bytes 2097152 | tf_op jit(solution)/shard_map/all_to_all | solution.py:15
  19.4 0.0 reduce-scatter.2.cloned.1.call-start
  19.5 0.0 copy-done.1
  19.5 0.0 copy-done.2
  19.5 0.1 broadcast_multiply_fusion
  19.6 27.2 %all-to-all-done = f32[32,32,256]{2,1,0:T(8,128)S(1)} async-done(((f32[32,32,256]{2,1,0:T(8,128)}), f32[32,32,256]{2,1,0:T(8,128)S(1)}, u32[]{:S(2)}, u32[]{:S(2)}) %all-to-all-start) | async-done | bytes 1048608 | tf_op jit(solution)/shard_map/all_to_all | solution.py:15
  46.8 6.6 %fusion = f32[1280,1024]{1,0:T(8,128)S(1)} fusion(f32[32,40,1024]{2,1,0:T(8,128)} %param.4, f32[1280,256]{1,0:T(8,128)S(1)} %bitcast.24, f32[1024,256]{1,0:T(8,128)S(1)} %bitcast.26), kind=kOutput, calls=%fused_computation.1 | convolution fusion | flops 4029153280 | bytes 12845056 | tf_op jit(solution)/shard_map/dot_general | solution.py:23
  53.5 0.0 copy-start
  53.5 2.3 copy-done
  55.8 9.6 %fusion.1 = f32[1024,256]{1,0:T(8,128)} fusion(f32[1280,1024]{1,0:T(8,128)S(1)} %fusion, f32[1280,256]{1,0:T(8,128)S(1)} %bitcast.25), kind=kOutput, calls=%fused_computation.5 | convolution fusion | flops 4026531840 | bytes 7602176 | tf_op jit(solution)/shard_map/dot_general | solution.py:25
  65.3 0.0 reduce-scatter.2.cloned.1.call-update
  65.4 0.2 all-reduce.3.cloned.1.call-start
  65.6 6.8 %multiply_reduce_fusion = (f32[256,40]{0,1:T(8,128)}, f32[32,40,256]{2,1,0:T(8,128)S(1)}) fusion(f32[256,32]{0,1:T(8,128)S(1)} %bitcast.30, f32[32,40,1024]{2,1,0:T(8,128)} %bitcast.23, f32[1024,256,1]{1,0,2:T(8,128)S(1)} %bitcast.27), kind=kOutput, calls=%fused_computation.2 | convolution fusion | flops 4027176960 | bytes 7675904 | tf_op jit(solution)/shard_map/dot_general | solution.py:26
  72.4 117.0 %reduce-scatter.2.cloned.1.call-done = f32[32,256]{1,0:T(8,128)} async-done(((f32[1024,256]{1,0:T(8,128)}), f32[32,256]{1,0:T(8,128)}) %reduce-scatter.2.cloned.1.call-update) | async-done | bytes 32784 | tf_op jit(solution)/shard_map/reduce_scatter | solution.py:32
  189.4 0.0 all-reduce.3.cloned.1.call-update
  189.4 0.1 multiply_reduce_fusion.1
  189.6 129.1 %psum.22 = f32[32,256]{1,0:T(8,128)} all-reduce(f32[32,256]{1,0:T(8,128)S(1)} %bitcast.31), channel_id=1, replica_groups=mesh['snap'=32,'var'=16] {'snap'}, use_global_device_ids=true, to_apply=%region_2.0 | all-reduce | flops 8192 | bytes 65536 | tf_op jit(solution)/shard_map/psum | solution.py:33
  318.7 12.9 %all-reduce.3.cloned.1.call-done = (f32[32,256]{1,0:T(8,128)}, f32[40,256]{1,0:T(8,128)}) async-done(((f32[32,256]{1,0:T(8,128)}, f32[40,256]{1,0:T(8,128)}), (f32[32,256]{1,0:T(8,128)}, f32[40,256]{1,0:T(8,128)})) %all-reduce.3.cloned.1.call-update) | async-done | bytes 73744 | tf_op jit(solution)/shard_map/psum | solution.py:31
  331.6 1.4 copy.23
  332.9 1.4 copy.24
Async XLA Ops:
  9.0 10.4 %copy-start.1 = (f32[40,256]{1,0:T(8,128)S(1)}, f32[40,256]{1,0:T(8,128)}, u32[]{:S(2)}) copy-start(f32[40,256]{1,0:T(8,128)} %param.7) | copy-start | bytes 122884
  9.0 10.4 %copy-start.2 = (f32[32,256]{1,0:T(8,128)S(1)}, f32[32,256]{1,0:T(8,128)}, u32[]{:S(2)}) copy-start(f32[32,256]{1,0:T(8,128)} %param.6) | copy-start | bytes 98308
  9.0 37.8 %all-to-all-start = ((f32[32,32,256]{2,1,0:T(8,128)}), f32[32,32,256]{2,1,0:T(8,128)S(1)}, u32[]{:S(2)}, u32[]{:S(2)}) async-start(f32[32,32,256]{2,1,0:T(8,128)} %stack.2), calls=%async_computation | async-start | bytes 2097152 | tf_op jit(solution)/shard_map/all_to_all | solution.py:15
  19.4 170.0 %reduce-scatter.2.cloned.1.call-start = ((), (), s32[]{:S(2)}) async-start(), calls=%async_computation.2 | async-start | bytes 1081344 | tf_op jit(solution)/shard_map/reduce_scatter | solution.py:32
  53.5 2.3 copy-start
  65.4 266.2 %all-reduce.3.cloned.1.call-start = ((), (), s32[]{:S(2)}) async-start(), calls=%async_computation.3 | async-start | bytes 147456 | tf_op jit(solution)/shard_map/psum | solution.py:31
Sparse Core Ops, SparseCore 0:
  65.5 123.8 reduce-scatter.1
  192.9 138.5 all-reduce.2
